TPU v7x, 32 devices: a whole 2x2x4 slice. The times are simulated.
32 devices in a mesh: sec: 4 (over x, core), sub: 8 (over z, y).
Axes of the slice: x: 2, y: 2, z: 4, core: 2. Of those that a mesh axis runs over, the one named last changes fastest.
Arguments:
- schur: bfloat16 [8, 1024, 1024], P('sub', 'sec'), may hold values from -0.1875 to 0.1875
- neumann: bfloat16 [8, 1024, 1024], P('sub', 'sec'), may hold values from -0.1875 to 0.1875
- constraint_weights: bfloat16 [8, 1024, 128], P('sub', 'sec'), may hold values from -0.1875 to 0.1875
- coarse_inverse: bfloat16 [8, 768, 768], P('sub', 'sec'), may hold values from -0.21875 to 0.21875
- solution: bfloat16 [8, 1024, 128], P('sub', 'sec'), may hold values from -6 to 6
- load: bfloat16 [8, 1024, 128], P('sub', 'sec'), may hold values from -6 to 6
- neighbours: int32 [8, 4], P('sub'), may hold values from 0 to 7, as said below
- face_index: int32 [8, 1024], P('sub', 'sec'), may hold values from 0 to 255, as said below
- coarse_dof: int32 [8, 128], P('sub'), may hold values from 0 to 6143, as said below
Outputs:
- precond: bfloat16 [8, 1024, 128], P('sub', 'sec')
- image: bfloat16 [8, 1024, 128], P('sub', 'sec')
Inputs may be any that keep to these rules, and one draw needn't show every extreme that they name: `neighbours`: the subdomain glued to face f of subdomain i is another subdomain whose column c // 1 is the column i // 1 of i or the one before or after it, cyclically over 8 columns. `face_index`: for each subdomain and face, the entries of the face's 256 unknowns are a permutation of 0 to 255. `coarse_dof`: constraint k of subdomain i maps to an unknown of the cluster of column i // 1 or of the column before or after it, cyclically. Each cluster has 64 coarse unknowns that are used, and each used unknown is the unknown of exactly two constraints.
All inputs are finite; a program needn't handle non-finite values.
Results may differ from a plain program's by a relative error of at most 0.0058.
Values may be sent and summed in bfloat16 or wider, within the bound.
No kernel may reach another device: no remote copies, remote signals or barrier semaphores. Data moves between devices by JAX's collectives and lax.ppermute only.
A program may use at most 64 MiB of HBM per device.

v0:
```python
import jax
import jax.numpy as jnp
from jax import lax
from jax.sharding import PartitionSpec as P

COLS = 128


def extended(cells, sides, width):
    for axis, dim in sides:
        count = lax.axis_size(axis)
        head = lax.slice_in_dim(cells, 0, width, axis=dim)
        tail = lax.slice_in_dim(cells, cells.shape[dim] - width, cells.shape[dim], axis=dim)
        cells = jnp.concatenate(
            [
                lax.ppermute(tail, axis, [(i, (i + 1) % count) for i in range(count)]),
                cells,
                lax.ppermute(head, axis, [((i + 1) % count, i) for i in range(count)]),
            ],
            axis=dim,
        )
    return cells


def row_folder(blocks, received):
    return jnp.einsum("srk,skc->src", blocks, received, preferred_element_type=jnp.float32)


def face_selector(face_index):
    face_len = face_index.shape[1]
    positions = lax.broadcasted_iota(jnp.int32, (face_index.shape[0], face_len, face_len), 2)
    return (face_index[:, :, None] == positions).astype(jnp.float32)


def pair_faces(own_field, rim_rows, rim_slot, selector):
    matched = jnp.take(rim_rows, rim_slot, axis=0)
    facing = jnp.einsum(
        "sde,sec->sdc",
        selector,
        matched,
        precision=lax.Precision.HIGHEST,
        preferred_element_type=jnp.float32,
    )
    return own_field + facing


def local(
    schur,
    neumann,
    constraint_weights,
    coarse_inverse,
    solution,
    load,
    neighbours,
    face_index,
    coarse_dof,
):
    sub_count = schur.shape[0]
    col_count = COLS
    coarse_len = coarse_inverse.shape[2]
    inverse_rows = coarse_inverse[0]
    my_column = lax.axis_index("sub")
    axis_len = lax.axis_size("sub")
    my_section = lax.axis_index("sec")
    nbr_ids = jnp.take(neighbours, my_section, axis=1)
    rim_slot = (nbr_ids // sub_count - my_column + 1) % axis_len * sub_count + nbr_ids % sub_count
    coarse_slot = (
        coarse_dof // coarse_len - my_column + 1
    ) % axis_len * coarse_len + coarse_dof % coarse_len
    selector = face_selector(face_index)
    dof_near = extended(coarse_dof, (("sub", 0),), sub_count)
    is_owned = dof_near // coarse_len == my_column
    owned_slot = jnp.where(is_owned, dof_near % coarse_len, coarse_len).reshape(-1)
    schur_iter = row_folder(schur, lax.all_gather(solution, "sec", axis=1, tiled=True))
    residual = load.astype(jnp.float32) - schur_iter
    residual_near = extended(residual, (("sub", 0),), sub_count)
    assembled = pair_faces(residual, residual_near, rim_slot, selector).astype(jnp.bfloat16)
    constraint_part = jnp.einsum(
        "srk,src->skc", constraint_weights, assembled, preferred_element_type=jnp.float32
    )
    constraint_values = lax.psum(constraint_part, "sec")
    value_near = extended(constraint_values, (("sub", 0),), sub_count)
    coarse_rhs = jax.ops.segment_sum(
        value_near.reshape(-1, col_count), owned_slot, num_segments=coarse_len + 1
    )[:coarse_len]
    coarse_piece = jnp.dot(
        inverse_rows, coarse_rhs.astype(jnp.bfloat16), preferred_element_type=jnp.float32
    ).astype(jnp.bfloat16)
    coarse_whole = lax.all_gather(coarse_piece, "sec", axis=0, tiled=True)
    coarse_near = extended(coarse_whole, (("sub", 0),), coarse_len)
    picked = jnp.take(coarse_near, coarse_slot.reshape(-1), axis=0).reshape(
        sub_count, -1, col_count
    )
    neumann_part = row_folder(neumann, lax.all_gather(assembled, "sec", axis=1, tiled=True))
    correction = neumann_part + jnp.einsum(
        "srk,skc->src", constraint_weights, picked, preferred_element_type=jnp.float32
    )
    correction_near = extended(correction, (("sub", 0),), sub_count)
    precond = (0.5 * pair_faces(correction, correction_near, rim_slot, selector)).astype(
        jnp.bfloat16
    )
    precond_image = row_folder(schur, lax.all_gather(precond, "sec", axis=1, tiled=True)).astype(
        jnp.bfloat16
    )
    return (precond, precond_image)


def solution(mesh):
    placed = (
        P("sub", "sec", None),
        P("sub", "sec", None),
        P("sub", "sec", None),
        P("sub", "sec", None),
        P("sub", "sec", None),
        P("sub", "sec", None),
        P("sub", None),
        P("sub", "sec"),
        P("sub", None),
    )
    return jax.shard_map(
        local,
        mesh=mesh,
        in_specs=placed,
        out_specs=(P("sub", "sec", None), P("sub", "sec", None)),
        check_vma=False,
    )
```

profile of v0, /device:TPU:0, one launch (start us, length us, event | category | flops | bytes accessed | tf_op | source)
XLA Modules:
  0.0 114.4 jit_solution(5369333689216355976)
XLA Ops:
  7.2 7.6 %all_gather.12 = bf16[1,1024,128]{2,1,0:T(8,128)(2,1)S(1)} all-gather(bf16[1,256,128]{2,1,0:T(8,128)(2,1)} %param.15), channel_id=1, replica_groups=mesh['sec'=4,'sub'=8] {'sec'}, dimensions={1}, use_global_device_ids=true | all-gather | bytes 327680 | tf_op jit(solution)/shard_map/all_gather | solution.py:74
  14.8 1.2 %fusion.2 = f32[1,256,128]{2,1,0:T(8,128)S(1)} fusion(bf16[1,256,1024]{2,1,0:T(8,128)(2,1)S(1)} %copy-done, bf16[1,1024,128]{2,1,0:T(8,128)(2,1)S(1)} %all_gather.12, bf16[1,256,128]{2,1,0:T(8,128)(2,1)} %param.16), kind=kOutput, calls=%fused_computation.8 | convolution fusion | flops 67174400 | bytes 983040 | tf_op jit(solution)/shard_map/srk,skc->src/dot_general | solution.py:26
  16.0 1.6 %collective-permute-start = (f32[1,256,128]{2,1,0:T(8,128)S(1)}, f32[1,256,128]{2,1,0:T(8,128)S(1)}, u32[]{:S(2)}, u32[]{:S(2)}) collective-permute-start(f32[1,256,128]{2,1,0:T(8,128)S(1)} %fusion.2), channel_id=1, source_target_pairs={{0,1},{1,2},{2,3},{3,4},{4,5},{5,6},{6,7},{7,0},{8,9},{9,10},{10,1... | collective-permute-start | bytes 393224 | tf_op jit(solution)/shard_map/ppermute | solution.py:16
  17.6 3.2 %collective-permute-start.1 = (f32[1,256,128]{2,1,0:T(8,128)S(1)}, f32[1,256,128]{2,1,0:T(8,128)S(1)}, u32[]{:S(2)}, u32[]{:S(2)}) collective-permute-start(f32[1,256,128]{2,1,0:T(8,128)S(1)} %fusion.2), channel_id=1, source_target_pairs={{1,0},{2,1},{3,2},{4,3},{5,4},{6,5},{7,6},{0,7},{9,8},{10,9},{11,1... | collective-permute-start | bytes 393224 | tf_op jit(solution)/shard_map/ppermute | solution.py:18
  20.8 4.7 %collective-permute-start.3 = (s32[1,128]{1,0:T(1,128)S(1)}, s32[1,128]{1,0:T(1,128)S(1)}, u32[]{:S(2)}, u32[]{:S(2)}) collective-permute-start(s32[1,128]{1,0:T(1,128)S(1)} %copy-done.4), channel_id=1, source_target_pairs={{1,0},{2,1},{3,2},{4,3},{5,4},{6,5},{7,6},{0,7},{9,8},{10,9},{11,1... | collective-permute-start | bytes 1544 | tf_op jit(solution)/shard_map/ppermute | solution.py:18
  25.5 0.6 constant_dynamic-slice_fusion
  27.4 0.8 convolution_bitcast_fusion.2
  28.3 33.1 %all-reduce.2.cloned.1.call-done = f32[1,128,128]{1,2,0:T(8,128)} async-done(((f32[1,128,128]{1,2,0:T(8,128)}), f32[1,128,128]{1,2,0:T(8,128)}) %all-reduce.2.cloned.1.call-update) | async-done | bytes 65552 | tf_op jit(solution)/shard_map/psum | solution.py:81
  61.4 1.5 %collective-permute-start.4 = (f32[1,128,128]{1,2,0:T(8,128)}, f32[1,128,128]{1,2,0:T(8,128)S(1)}, u32[]{:S(2)}, u32[]{:S(2)}) collective-permute-start(f32[1,128,128]{1,2,0:T(8,128)} %all-reduce.2.cloned.1.call-done), channel_id=1, source_target_pairs={{0,1},{1,2},{2,3},{3,4},{4,5},{5,6},{6,7},{7,0},{8,9},{9,10},{10,1... | collective-permute-start | bytes 196616 | tf_op jit(solution)/shard_map/ppermute | solution.py:16
  62.9 3.2 %collective-permute-start.5 = (f32[1,128,128]{1,2,0:T(8,128)}, f32[1,128,128]{1,2,0:T(8,128)S(1)}, u32[]{:S(2)}, u32[]{:S(2)}) collective-permute-start(f32[1,128,128]{1,2,0:T(8,128)} %all-reduce.2.cloned.1.call-done), channel_id=1, source_target_pairs={{1,0},{2,1},{3,2},{4,3},{5,4},{6,5},{7,6},{0,7},{9,8},{10,9},{11,1... | collective-permute-start | bytes 196616 | tf_op jit(solution)/shard_map/ppermute | solution.py:18
  66.2 2.4 %collective-permute-done.4 = f32[1,128,128]{1,2,0:T(8,128)S(1)} collective-permute-done((f32[1,128,128]{1,2,0:T(8,128)}, f32[1,128,128]{1,2,0:T(8,128)S(1)}, u32[]{:S(2)}, u32[]{:S(2)}) %collective-permute-start.4) | collective-permute-done | bytes 65568 | tf_op jit(solution)/shard_map/ppermute | solution.py:16
  68.6 0.9 pad_maximum_fusion.1
  69.6 2.5 %scatter_custom_fusion = f32[769,128]{1,0:T(8,128)S(1)} fusion(s32[384]{0:T(512)S(1)} %fusion.45, f32[384,128]{1,0:T(8,128)S(1)} %bitcast.118, f32[]{:T(128)} %constant.133.clone.1), kind=kCustom, calls=%fused_computation.32 | custom fusion | flops 49152 | bytes 393732 | tf_op jit(solution)/shard_map/scatter-add | solution.py:83
  72.3 5.6 %all_gather.14 = bf16[768,128]{1,0:T(8,128)(2,1)S(1)} all-gather(bf16[192,128]{1,0:T(8,128)(2,1)S(1)} %fusion.6), channel_id=1, replica_groups=mesh['sec'=4,'sub'=8] {'sec'}, dimensions={0}, use_global_device_ids=true | all-gather | bytes 245760 | tf_op jit(solution)/shard_map/all_gather | solution.py:89
  77.9 1.1 collective-permute-start.6
  79.0 3.6 %collective-permute-start.7 = (bf16[768,128]{1,0:T(8,128)(2,1)S(1)}, bf16[768,128]{1,0:T(8,128)(2,1)S(1)}, u32[]{:S(2)}, u32[]{:S(2)}) collective-permute-start(bf16[768,128]{1,0:T(8,128)(2,1)S(1)} %all_gather.14), channel_id=1, source_target_pairs={{1,0},{2,1},{3,2},{4,3},{5,4},{6,5},{7,6},{0,7},{9,8},{10,9},{11,1... | collective-permute-start | bytes 589832 | tf_op jit(solution)/shard_map/ppermute | solution.py:18
  82.6 5.8 %all_gather.13 = bf16[1,1024,128]{2,1,0:T(8,128)(2,1)S(1)} all-gather(bf16[1,256,128]{2,1,0:T(8,128)(2,1)S(1)} %fusion.4), channel_id=1, replica_groups=mesh['sec'=4,'sub'=8] {'sec'}, dimensions={1}, use_global_device_ids=true | all-gather | bytes 327680 | tf_op jit(solution)/shard_map/all_gather | solution.py:94
  88.4 1.7 %collective-permute-done.7 = bf16[768,128]{1,0:T(8,128)(2,1)S(1)} collective-permute-done((bf16[768,128]{1,0:T(8,128)(2,1)S(1)}, bf16[768,128]{1,0:T(8,128)(2,1)S(1)}, u32[]{:S(2)}, u32[]{:S(2)}) %collective-permute-start.7) | collective-permute-done | bytes 196640 | tf_op jit(solution)/shard_map/ppermute | solution.py:18
  90.1 0.7 gather_fusion
  91.8 4.4 %collective-permute-start.9 = (f32[1,256,128]{1,2,0:T(8,128)S(1)}, f32[1,256,128]{1,2,0:T(8,128)S(1)}, u32[]{:S(2)}, u32[]{:S(2)}) collective-permute-start(f32[1,256,128]{1,2,0:T(8,128)S(1)} %bitcast.115), channel_id=1, source_target_pairs={{1,0},{2,1},{3,2},{4,3},{5,4},{6,5},{7,6},{0,7},{9,8},{10,9},{11,1... | collective-permute-start | bytes 393224 | tf_op jit(solution)/shard_map/ppermute | solution.py:18
  96.2 2.9 %collective-permute-done.8 = f32[1,256,128]{1,2,0:T(8,128)S(1)} collective-permute-done((f32[1,256,128]{1,2,0:T(8,128)S(1)}, f32[1,256,128]{1,2,0:T(8,128)S(1)}, u32[]{:S(2)}, u32[]{:S(2)}) %collective-permute-start.8) | collective-permute-done | bytes 131104 | tf_op jit(solution)/shard_map/ppermute | solution.py:16
  100.0 5.8 %all-gather = bf16[1024,128]{0,1:T(8,128)(2,1)S(1)} all-gather(bf16[256,128]{0,1:T(8,128)(2,1)S(1)} %fusion.3), channel_id=2, replica_groups=mesh['sec'=4,'sub'=8] {'sec'}, dimensions={0}, use_global_device_ids=true | all-gather | bytes 327680 | tf_op jit(solution)/shard_map/all_gather | solution.py:102
  106.1 0.7 copy.17
  106.8 0.7 copy.16
  (39 shorter events, 3.1 us)
Async XLA Ops:
  7.2 7.6 %copy-start = (bf16[1,256,1024]{2,1,0:T(8,128)(2,1)S(1)}, bf16[1,256,1024]{2,1,0:T(8,128)(2,1)}, u32[]{:S(2)}) copy-start(bf16[1,256,1024]{2,1,0:T(8,128)(2,1)} %param.11) | copy-start | bytes 1572868
  7.2 13.6 %copy-start.4 = (s32[1,128]{1,0:T(1,128)S(1)}, s32[1,128]{1,0:T(1,128)}, u32[]{:S(2)}) copy-start(s32[1,128]{1,0:T(1,128)} %param.19) | copy-start | bytes 1540
  7.2 18.3 %copy-start.6 = (s32[1,4]{1,0:T(1,128)S(1)}, s32[1,4]{1,0:T(1,128)}, u32[]{:S(2)}) copy-start(s32[1,4]{1,0:T(1,128)} %param.17) | copy-start | bytes 52
  7.2 54.2 %all-reduce.2.cloned.1.call-start = ((), (), s32[]{:S(2)}) async-start(), calls=%async_computation | async-start | bytes 131072 | tf_op jit(solution)/shard_map/psum | solution.py:81
  14.8 12.3 %copy-start.5 = (s32[1,256]{1,0:T(1,128)S(1)}, s32[1,256]{1,0:T(1,128)}, u32[]{:S(2)}) copy-start(s32[1,256]{1,0:T(1,128)} %param.18) | copy-start | bytes 3076
  14.8 12.6 %copy-start.3 = (bf16[1,256,128]{2,1,0:T(8,128)(2,1)S(1)}, bf16[1,256,128]{2,1,0:T(8,128)(2,1)}, u32[]{:S(2)}) copy-start(bf16[1,256,128]{2,1,0:T(8,128)(2,1)} %param.13) | copy-start | bytes 196612
  16.0 11.1 %collective-permute-start = (f32[1,256,128]{2,1,0:T(8,128)S(1)}, f32[1,256,128]{2,1,0:T(8,128)S(1)}, u32[]{:S(2)}, u32[]{:S(2)}) collective-permute-start(f32[1,256,128]{2,1,0:T(8,128)S(1)} %fusion.2), channel_id=1, source_target_pairs={{0,1},{1,2},{2,3},{3,4},{4,5},{5,6},{6,7},{7,0},{8,9},{9,10},{10,1... | collective-permute-start | bytes 393224 | tf_op jit(solution)/shard_map/ppermute | solution.py:16
  17.6 9.5 %collective-permute-start.1 = (f32[1,256,128]{2,1,0:T(8,128)S(1)}, f32[1,256,128]{2,1,0:T(8,128)S(1)}, u32[]{:S(2)}, u32[]{:S(2)}) collective-permute-start(f32[1,256,128]{2,1,0:T(8,128)S(1)} %fusion.2), channel_id=1, source_target_pairs={{1,0},{2,1},{3,2},{4,3},{5,4},{6,5},{7,6},{0,7},{9,8},{10,9},{11,1... | collective-permute-start | bytes 393224 | tf_op jit(solution)/shard_map/ppermute | solution.py:18
  20.8 6.3 %collective-permute-start.2 = (s32[1,128]{1,0:T(1,128)S(1)}, s32[1,128]{1,0:T(1,128)S(1)}, u32[]{:S(2)}, u32[]{:S(2)}) collective-permute-start(s32[1,128]{1,0:T(1,128)S(1)} %copy-done.4), channel_id=1, source_target_pairs={{0,1},{1,2},{2,3},{3,4},{4,5},{5,6},{6,7},{7,0},{8,9},{9,10},{10,1... | collective-permute-start | bytes 1544 | tf_op jit(solution)/shard_map/ppermute | solution.py:16
  20.8 6.3 %collective-permute-start.3 = (s32[1,128]{1,0:T(1,128)S(1)}, s32[1,128]{1,0:T(1,128)S(1)}, u32[]{:S(2)}, u32[]{:S(2)}) collective-permute-start(s32[1,128]{1,0:T(1,128)S(1)} %copy-done.4), channel_id=1, source_target_pairs={{1,0},{2,1},{3,2},{4,3},{5,4},{6,5},{7,6},{0,7},{9,8},{10,9},{11,1... | collective-permute-start | bytes 1544 | tf_op jit(solution)/shard_map/ppermute | solution.py:18
  61.4 7.2 %collective-permute-start.4 = (f32[1,128,128]{1,2,0:T(8,128)}, f32[1,128,128]{1,2,0:T(8,128)S(1)}, u32[]{:S(2)}, u32[]{:S(2)}) collective-permute-start(f32[1,128,128]{1,2,0:T(8,128)} %all-reduce.2.cloned.1.call-done), channel_id=1, source_target_pairs={{0,1},{1,2},{2,3},{3,4},{4,5},{5,6},{6,7},{7,0},{8,9},{9,10},{10,1... | collective-permute-start | bytes 196616 | tf_op jit(solution)/shard_map/ppermute | solution.py:16
  62.9 5.7 %collective-permute-start.5 = (f32[1,128,128]{1,2,0:T(8,128)}, f32[1,128,128]{1,2,0:T(8,128)S(1)}, u32[]{:S(2)}, u32[]{:S(2)}) collective-permute-start(f32[1,128,128]{1,2,0:T(8,128)} %all-reduce.2.cloned.1.call-done), channel_id=1, source_target_pairs={{1,0},{2,1},{3,2},{4,3},{5,4},{6,5},{7,6},{0,7},{9,8},{10,9},{11,1... | collective-permute-start | bytes 196616 | tf_op jit(solution)/shard_map/ppermute | solution.py:18
  66.1 5.9 %copy-start.2 = (bf16[1,192,768]{2,1,0:T(8,128)(2,1)S(1)}, bf16[1,192,768]{2,1,0:T(8,128)(2,1)}, u32[]{:S(2)}) copy-start(bf16[1,192,768]{2,1,0:T(8,128)(2,1)} %param.14) | copy-start | bytes 884740
  77.9 10.5 %collective-permute-start.6 = (bf16[768,128]{1,0:T(8,128)(2,1)S(1)}, bf16[768,128]{1,0:T(8,128)(2,1)S(1)}, u32[]{:S(2)}, u32[]{:S(2)}) collective-permute-start(bf16[768,128]{1,0:T(8,128)(2,1)S(1)} %all_gather.14), channel_id=1, source_target_pairs={{0,1},{1,2},{2,3},{3,4},{4,5},{5,6},{6,7},{7,0},{8,9},{9,10},{10,1... | collective-permute-start | bytes 589832 | tf_op jit(solution)/shard_map/ppermute | solution.py:16
  79.0 11.1 %collective-permute-start.7 = (bf16[768,128]{1,0:T(8,128)(2,1)S(1)}, bf16[768,128]{1,0:T(8,128)(2,1)S(1)}, u32[]{:S(2)}, u32[]{:S(2)}) collective-permute-start(bf16[768,128]{1,0:T(8,128)(2,1)S(1)} %all_gather.14), channel_id=1, source_target_pairs={{1,0},{2,1},{3,2},{4,3},{5,4},{6,5},{7,6},{0,7},{9,8},{10,9},{11,1... | collective-permute-start | bytes 589832 | tf_op jit(solution)/shard_map/ppermute | solution.py:18
  88.4 2.7 %copy-start.1 = (bf16[1,256,1024]{2,1,0:T(8,128)(2,1)S(1)}, bf16[1,256,1024]{2,1,0:T(8,128)(2,1)}, u32[]{:S(2)}) copy-start(bf16[1,256,1024]{2,1,0:T(8,128)(2,1)} %param.12) | copy-start | bytes 1572868
  91.4 7.7 %collective-permute-start.8 = (f32[1,256,128]{1,2,0:T(8,128)S(1)}, f32[1,256,128]{1,2,0:T(8,128)S(1)}, u32[]{:S(2)}, u32[]{:S(2)}) collective-permute-start(f32[1,256,128]{1,2,0:T(8,128)S(1)} %bitcast.114), channel_id=1, source_target_pairs={{0,1},{1,2},{2,3},{3,4},{4,5},{5,6},{6,7},{7,0},{8,9},{9,10},{10,1... | collective-permute-start | bytes 393224 | tf_op jit(solution)/shard_map/ppermute | solution.py:16
  91.8 7.8 %collective-permute-start.9 = (f32[1,256,128]{1,2,0:T(8,128)S(1)}, f32[1,256,128]{1,2,0:T(8,128)S(1)}, u32[]{:S(2)}, u32[]{:S(2)}) collective-permute-start(f32[1,256,128]{1,2,0:T(8,128)S(1)} %bitcast.115), channel_id=1, source_target_pairs={{1,0},{2,1},{3,2},{4,3},{5,4},{6,5},{7,6},{0,7},{9,8},{10,9},{11,1... | collective-permute-start | bytes 393224 | tf_op jit(solution)/shard_map/ppermute | solution.py:18
Sparse Core Ops, SparseCore 0:
  28.4 32.9 all-reduce.1
where the time goes:
time: 115 us; the launch traced here: 114 us
  waiting for transfers between devices  40.9 us (36%)
  blocking collectives  24.7 us (21%)
  starting transfers between devices  23.8 us (21%)
  between operations  14.9 us (13%)
  matrix products  3.78 us (3%)
  other arithmetic  3.45 us (3%)
  local copies, waits for them, and re-layouts  2.92 us (3%)
    psum x1, waiting for transfers between devices, local(): constraint_values = lax.psum(constraint_part, 'sec')  33.1 us
    ppermute x5, starting transfers between devices, extended(): lax.ppermute(head, axis, [((i + 1) % count, i) for i in range(count)])  19.2 us
    all_gather x1, blocking collectives, local(): lax.all_gather(solution, 'sec', axis=1, tiled=True)  7.57 us
    all_gather x1, blocking collectives, local(): lax.all_gather(precond, 'sec', axis=1, tiled=True)  5.78 us
    all_gather x1, blocking collectives, local(): lax.all_gather(assembled, 'sec', axis=1, tiled=True)  5.76 us
    all_gather x1, blocking collectives, local(): coarse_whole = lax.all_gather(coarse_piece, 'sec', axis=0, tiled=True)  5.6 us
    ppermute x5, waiting for transfers between devices, extended(): lax.ppermute(tail, axis, [(i, (i + 1) % count) for i in range(count)])  5.58 us
    ppermute x5, starting transfers between devices, extended(): lax.ppermute(tail, axis, [(i, (i + 1) % count) for i in range(count)])  4.55 us
  transfers between devices with their start and end apart: 11, of which 6 were waited for; matrix products, arithmetic and copies ran while one was open for 1% of the time, Pallas kernels for 0%

commit v1 on v0

--- a/solution.py
+++ b/solution.py
@@ -78,7 +78,7 @@
     constraint_part = jnp.einsum(
         "srk,src->skc", constraint_weights, assembled, preferred_element_type=jnp.float32
     )
-    constraint_values = lax.psum(constraint_part, "sec")
+    constraint_values = jnp.sum(lax.all_gather(constraint_part, "sec"), axis=0)
     value_near = extended(constraint_values, (("sub", 0),), sub_count)
     coarse_rhs = jax.ops.segment_sum(
         value_near.reshape(-1, col_count), owned_slot, num_segments=coarse_len + 1

time: 115 us -> 71.9 us (0.63)
  waiting for transfers between devices: 40.9 us -> 6.95 us
  between operations: 14.9 us -> 1.51 us
  blocking collectives: 24.7 us -> 30.5 us
    psum x1 -> x0, waiting for transfers between devices: 33.1 us -> none  [local(): constraint_values = lax.psum(constraint_part, 'sec')]
    all_gather x0 -> x1, blocking collectives: none -> 5.78 us  [local(): constraint_values = jnp.sum(lax.all_gather(constraint_part, 'sec'), axis=0)]
    ppermute x5, starting transfers between devices: 19.2 us -> 21.8 us  [extended(): lax.ppermute(head, axis, [((i + 1) % count, i) for i in range(count)])]
    ppermute x5, starting transfers between devices: 4.55 us -> 2 us  [extended(): lax.ppermute(tail, axis, [(i, (i + 1) % count) for i in range(count)])]
  transfers between devices with their start and end apart: 11 -> 10, of which waited for: 6 -> 5; matrix products, arithmetic and copies ran while one was open for 1% -> 1% of each run, Pallas kernels for 0% -> 0%
where the time goes in v1:
time: 71.9 us; the launch traced here: 71.7 us
  blocking collectives  30.5 us (42%)
  starting transfers between devices  23.8 us (33%)
  waiting for transfers between devices  6.95 us (10%)
  matrix products  3.14 us (4%)
  local copies, waits for them, and re-layouts  3.01 us (4%)
  other arithmetic  2.77 us (4%)
  between operations  1.51 us (2%)
    ppermute x5, starting transfers between devices, extended(): lax.ppermute(head, axis, [((i + 1) % count, i) for i in range(count)])  21.8 us
    all_gather x1, blocking collectives, local(): lax.all_gather(solution, 'sec', axis=1, tiled=True)  7.57 us
    all_gather x1, blocking collectives, local(): constraint_values = jnp.sum(lax.all_gather(constraint_part, 'sec'), axis=0)  5.78 us
    all_gather x1, blocking collectives, local(): lax.all_gather(precond, 'sec', axis=1, tiled=True)  5.78 us
    ppermute x5, waiting for transfers between devices, extended(): lax.ppermute(tail, axis, [(i, (i + 1) % count) for i in range(count)])  5.77 us
    all_gather x1, blocking collectives, local(): lax.all_gather(assembled, 'sec', axis=1, tiled=True)  5.76 us
    all_gather x1, blocking collectives, local(): coarse_whole = lax.all_gather(coarse_piece, 'sec', axis=0, tiled=True)  5.6 us
    scatter-add x1, other arithmetic, local(): jax.ops.segment_sum(value_near.reshape(-1, col_count), owned_slot, num_se...  2.46 us
  transfers between devices with their start and end apart: 10, of which 5 were waited for; matrix products, arithmetic and copies ran while one was open for 1% of the time, Pallas kernels for 0%

profile of v1, /device:TPU:0, one launch (start us, length us, event | category | flops | bytes accessed | tf_op | source)
XLA Modules:
  0.0 71.7 jit_solution(14184764025865215763)
XLA Ops:
  0.7 7.6 %all_gather.18 = bf16[1,1024,128]{2,1,0:T(8,128)(2,1)S(1)} all-gather(bf16[1,256,128]{2,1,0:T(8,128)(2,1)} %param.15), channel_id=1, replica_groups=mesh['sec'=4,'sub'=8] {'sec'}, dimensions={1}, use_global_device_ids=true | all-gather | bytes 327680 | tf_op jit(solution)/shard_map/all_gather | solution.py:74
  8.2 1.2 %fusion.2 = f32[1,256,128]{2,1,0:T(8,128)S(1)} fusion(bf16[1,256,1024]{2,1,0:T(8,128)(2,1)S(1)} %copy-done, bf16[1,1024,128]{2,1,0:T(8,128)(2,1)S(1)} %all_gather.18, bf16[1,256,128]{2,1,0:T(8,128)(2,1)} %param.16), kind=kOutput, calls=%fused_computation.8 | convolution fusion | flops 67174400 | bytes 983040 | tf_op jit(solution)/shard_map/srk,skc->src/dot_general | solution.py:26
  9.4 1.6 %collective-permute-start = (f32[1,256,128]{2,1,0:T(8,128)S(1)}, f32[1,256,128]{2,1,0:T(8,128)S(1)}, u32[]{:S(2)}, u32[]{:S(2)}) collective-permute-start(f32[1,256,128]{2,1,0:T(8,128)S(1)} %fusion.2), channel_id=1, source_target_pairs={{0,1},{1,2},{2,3},{3,4},{4,5},{5,6},{6,7},{7,0},{8,9},{9,10},{10,1... | collective-permute-start | bytes 393224 | tf_op jit(solution)/shard_map/ppermute | solution.py:16
  11.0 3.2 %collective-permute-start.1 = (f32[1,256,128]{2,1,0:T(8,128)S(1)}, f32[1,256,128]{2,1,0:T(8,128)S(1)}, u32[]{:S(2)}, u32[]{:S(2)}) collective-permute-start(f32[1,256,128]{2,1,0:T(8,128)S(1)} %fusion.2), channel_id=1, source_target_pairs={{1,0},{2,1},{3,2},{4,3},{5,4},{6,5},{7,6},{0,7},{9,8},{10,9},{11,1... | collective-permute-start | bytes 393224 | tf_op jit(solution)/shard_map/ppermute | solution.py:18
  14.2 4.7 %collective-permute-start.3 = (s32[1,128]{1,0:T(1,128)S(1)}, s32[1,128]{1,0:T(1,128)S(1)}, u32[]{:S(2)}, u32[]{:S(2)}) collective-permute-start(s32[1,128]{1,0:T(1,128)S(1)} %copy-done.4), channel_id=1, source_target_pairs={{1,0},{2,1},{3,2},{4,3},{5,4},{6,5},{7,6},{0,7},{9,8},{10,9},{11,1... | collective-permute-start | bytes 1544 | tf_op jit(solution)/shard_map/ppermute | solution.py:18
  18.9 0.6 constant_dynamic-slice_fusion
  21.0 5.8 %all-gather = f32[512,128]{0,1:T(8,128)S(1)} all-gather(f32[128,128]{0,1:T(8,128)S(1)} %convolution_bitcast_fusion.2), channel_id=2, replica_groups=mesh['sec'=4,'sub'=8] {'sec'}, dimensions={0}, use_global_device_ids=true | all-gather | bytes 327680 | tf_op jit(solution)/shard_map/all_gather | solution.py:81
  27.1 4.8 %collective-permute-start.5 = (f32[1,128,128]{1,2,0:T(8,128)S(1)}, f32[1,128,128]{1,2,0:T(8,128)S(1)}, u32[]{:S(2)}, u32[]{:S(2)}) collective-permute-start(f32[1,128,128]{1,2,0:T(8,128)S(1)} %bitcast.120), channel_id=1, source_target_pairs={{1,0},{2,1},{3,2},{4,3},{5,4},{6,5},{7,6},{0,7},{9,8},{10,9},{11,1... | collective-permute-start | bytes 196616 | tf_op jit(solution)/shard_map/ppermute | solution.py:18
  32.0 2.5 %collective-permute-done.4 = f32[1,128,128]{1,2,0:T(8,128)S(1)} collective-permute-done((f32[1,128,128]{1,2,0:T(8,128)S(1)}, f32[1,128,128]{1,2,0:T(8,128)S(1)}, u32[]{:S(2)}, u32[]{:S(2)}) %collective-permute-start.4) | collective-permute-done | bytes 65568 | tf_op jit(solution)/shard_map/ppermute | solution.py:16
  34.6 2.5 %scatter_custom_fusion = f32[769,128]{1,0:T(8,128)S(1)} fusion(s32[384]{0:T(512)S(1)} %fusion.45, f32[384,128]{1,0:T(8,128)S(1)} %bitcast.122, f32[]{:T(128)} %constant.134.clone.1), kind=kCustom, calls=%fused_computation.32 | custom fusion | flops 49152 | bytes 393732 | tf_op jit(solution)/shard_map/scatter-add | solution.py:83
  37.3 5.6 %all_gather.22 = bf16[768,128]{1,0:T(8,128)(2,1)S(1)} all-gather(bf16[192,128]{1,0:T(8,128)(2,1)S(1)} %fusion.6), channel_id=1, replica_groups=mesh['sec'=4,'sub'=8] {'sec'}, dimensions={0}, use_global_device_ids=true | all-gather | bytes 245760 | tf_op jit(solution)/shard_map/all_gather | solution.py:89
  42.9 4.7 %collective-permute-start.7 = (bf16[768,128]{1,0:T(8,128)(2,1)S(1)}, bf16[768,128]{1,0:T(8,128)(2,1)S(1)}, u32[]{:S(2)}, u32[]{:S(2)}) collective-permute-start(bf16[768,128]{1,0:T(8,128)(2,1)S(1)} %all_gather.22), channel_id=1, source_target_pairs={{1,0},{2,1},{3,2},{4,3},{5,4},{6,5},{7,6},{0,7},{9,8},{10,9},{11,1... | collective-permute-start | bytes 589832 | tf_op jit(solution)/shard_map/ppermute | solution.py:18
  47.6 5.8 %all_gather.19 = bf16[1,1024,128]{2,1,0:T(8,128)(2,1)S(1)} all-gather(bf16[1,256,128]{2,1,0:T(8,128)(2,1)S(1)} %fusion.4), channel_id=1, replica_groups=mesh['sec'=4,'sub'=8] {'sec'}, dimensions={1}, use_global_device_ids=true | all-gather | bytes 327680 | tf_op jit(solution)/shard_map/all_gather | solution.py:94
  53.4 0.9 %collective-permute-done.7 = bf16[768,128]{1,0:T(8,128)(2,1)S(1)} collective-permute-done((bf16[768,128]{1,0:T(8,128)(2,1)S(1)}, bf16[768,128]{1,0:T(8,128)(2,1)S(1)}, u32[]{:S(2)}, u32[]{:S(2)}) %collective-permute-start.7) | collective-permute-done | bytes 196640 | tf_op jit(solution)/shard_map/ppermute | solution.py:18
  54.3 0.7 gather_fusion
  55.3 0.3 convolution_add_fusion
  55.6 0.3 collective-permute-start.8
  56.0 4.4 %collective-permute-start.9 = (f32[1,256,128]{1,2,0:T(8,128)S(1)}, f32[1,256,128]{1,2,0:T(8,128)S(1)}, u32[]{:S(2)}, u32[]{:S(2)}) collective-permute-start(f32[1,256,128]{1,2,0:T(8,128)S(1)} %bitcast.116), channel_id=1, source_target_pairs={{1,0},{2,1},{3,2},{4,3},{5,4},{6,5},{7,6},{0,7},{9,8},{10,9},{11,1... | collective-permute-start | bytes 393224 | tf_op jit(solution)/shard_map/ppermute | solution.py:18
  60.4 3.0 %collective-permute-done.8 = f32[1,256,128]{1,2,0:T(8,128)S(1)} collective-permute-done((f32[1,256,128]{1,2,0:T(8,128)S(1)}, f32[1,256,128]{1,2,0:T(8,128)S(1)}, u32[]{:S(2)}, u32[]{:S(2)}) %collective-permute-start.8) | collective-permute-done | bytes 131104 | tf_op jit(solution)/shard_map/ppermute | solution.py:16
  63.7 0.4 fusion.3
  64.1 5.8 %all-gather.1 = bf16[1024,128]{0,1:T(8,128)(2,1)S(1)} all-gather(bf16[256,128]{0,1:T(8,128)(2,1)S(1)} %fusion.3), channel_id=3, replica_groups=mesh['sec'=4,'sub'=8] {'sec'}, dimensions={0}, use_global_device_ids=true | all-gather | bytes 327680 | tf_op jit(solution)/shard_map/all_gather | solution.py:102
  69.9 0.3 fusion.5
  70.2 0.7 %copy.23 = bf16[1,256,128]{2,1,0:T(8,128)(2,1)} copy(bf16[1,256,128]{1,2,0:T(8,128)(2,1)S(1)} %fusion.5) | data formatting | bytes 131072
  71.0 0.7 %copy.22 = bf16[1,256,128]{2,1,0:T(8,128)(2,1)} copy(bf16[1,256,128]{1,2,0:T(8,128)(2,1)S(1)} %bitcast.118) | data formatting | bytes 131072
  (39 shorter events, 2.1 us)
Async XLA Ops:
  0.6 7.6 %copy-start = (bf16[1,256,1024]{2,1,0:T(8,128)(2,1)S(1)}, bf16[1,256,1024]{2,1,0:T(8,128)(2,1)}, u32[]{:S(2)}) copy-start(bf16[1,256,1024]{2,1,0:T(8,128)(2,1)} %param.11) | copy-start | bytes 1572868
  0.6 13.5 %copy-start.4 = (s32[1,128]{1,0:T(1,128)S(1)}, s32[1,128]{1,0:T(1,128)}, u32[]{:S(2)}) copy-start(s32[1,128]{1,0:T(1,128)} %param.19) | copy-start | bytes 1540
  0.7 18.3 %copy-start.6 = (s32[1,4]{1,0:T(1,128)S(1)}, s32[1,4]{1,0:T(1,128)}, u32[]{:S(2)}) copy-start(s32[1,4]{1,0:T(1,128)} %param.17) | copy-start | bytes 52
  8.2 12.3 %copy-start.5 = (s32[1,256]{1,0:T(1,128)S(1)}, s32[1,256]{1,0:T(1,128)}, u32[]{:S(2)}) copy-start(s32[1,256]{1,0:T(1,128)} %param.18) | copy-start | bytes 3076
  8.2 12.6 %copy-start.3 = (bf16[1,256,128]{2,1,0:T(8,128)(2,1)S(1)}, bf16[1,256,128]{2,1,0:T(8,128)(2,1)}, u32[]{:S(2)}) copy-start(bf16[1,256,128]{2,1,0:T(8,128)(2,1)} %param.13) | copy-start | bytes 196612
  9.4 11.1 %collective-permute-start = (f32[1,256,128]{2,1,0:T(8,128)S(1)}, f32[1,256,128]{2,1,0:T(8,128)S(1)}, u32[]{:S(2)}, u32[]{:S(2)}) collective-permute-start(f32[1,256,128]{2,1,0:T(8,128)S(1)} %fusion.2), channel_id=1, source_target_pairs={{0,1},{1,2},{2,3},{3,4},{4,5},{5,6},{6,7},{7,0},{8,9},{9,10},{10,1... | collective-permute-start | bytes 393224 | tf_op jit(solution)/shard_map/ppermute | solution.py:16
  11.0 9.5 %collective-permute-start.1 = (f32[1,256,128]{2,1,0:T(8,128)S(1)}, f32[1,256,128]{2,1,0:T(8,128)S(1)}, u32[]{:S(2)}, u32[]{:S(2)}) collective-permute-start(f32[1,256,128]{2,1,0:T(8,128)S(1)} %fusion.2), channel_id=1, source_target_pairs={{1,0},{2,1},{3,2},{4,3},{5,4},{6,5},{7,6},{0,7},{9,8},{10,9},{11,1... | collective-permute-start | bytes 393224 | tf_op jit(solution)/shard_map/ppermute | solution.py:18
  14.2 6.3 %collective-permute-start.2 = (s32[1,128]{1,0:T(1,128)S(1)}, s32[1,128]{1,0:T(1,128)S(1)}, u32[]{:S(2)}, u32[]{:S(2)}) collective-permute-start(s32[1,128]{1,0:T(1,128)S(1)} %copy-done.4), channel_id=1, source_target_pairs={{0,1},{1,2},{2,3},{3,4},{4,5},{5,6},{6,7},{7,0},{8,9},{9,10},{10,1... | collective-permute-start | bytes 1544 | tf_op jit(solution)/shard_map/ppermute | solution.py:16
  14.2 6.3 %collective-permute-start.3 = (s32[1,128]{1,0:T(1,128)S(1)}, s32[1,128]{1,0:T(1,128)S(1)}, u32[]{:S(2)}, u32[]{:S(2)}) collective-permute-start(s32[1,128]{1,0:T(1,128)S(1)} %copy-done.4), channel_id=1, source_target_pairs={{1,0},{2,1},{3,2},{4,3},{5,4},{6,5},{7,6},{0,7},{9,8},{10,9},{11,1... | collective-permute-start | bytes 1544 | tf_op jit(solution)/shard_map/ppermute | solution.py:18
  27.1 7.4 %collective-permute-start.4 = (f32[1,128,128]{1,2,0:T(8,128)S(1)}, f32[1,128,128]{1,2,0:T(8,128)S(1)}, u32[]{:S(2)}, u32[]{:S(2)}) collective-permute-start(f32[1,128,128]{1,2,0:T(8,128)S(1)} %bitcast.119), channel_id=1, source_target_pairs={{0,1},{1,2},{2,3},{3,4},{4,5},{5,6},{6,7},{7,0},{8,9},{9,10},{10,1... | collective-permute-start | bytes 196616 | tf_op jit(solution)/shard_map/ppermute | solution.py:16
  27.1 7.3 %collective-permute-start.5 = (f32[1,128,128]{1,2,0:T(8,128)S(1)}, f32[1,128,128]{1,2,0:T(8,128)S(1)}, u32[]{:S(2)}, u32[]{:S(2)}) collective-permute-start(f32[1,128,128]{1,2,0:T(8,128)S(1)} %bitcast.120), channel_id=1, source_target_pairs={{1,0},{2,1},{3,2},{4,3},{5,4},{6,5},{7,6},{0,7},{9,8},{10,9},{11,1... | collective-permute-start | bytes 196616 | tf_op jit(solution)/shard_map/ppermute | solution.py:18
  31.9 5.1 %copy-start.2 = (bf16[1,192,768]{2,1,0:T(8,128)(2,1)S(1)}, bf16[1,192,768]{2,1,0:T(8,128)(2,1)}, u32[]{:S(2)}) copy-start(bf16[1,192,768]{2,1,0:T(8,128)(2,1)} %param.14) | copy-start | bytes 884740
  42.9 10.5 %collective-permute-start.6 = (bf16[768,128]{1,0:T(8,128)(2,1)S(1)}, bf16[768,128]{1,0:T(8,128)(2,1)S(1)}, u32[]{:S(2)}, u32[]{:S(2)}) collective-permute-start(bf16[768,128]{1,0:T(8,128)(2,1)S(1)} %all_gather.22), channel_id=1, source_target_pairs={{0,1},{1,2},{2,3},{3,4},{4,5},{5,6},{6,7},{7,0},{8,9},{9,10},{10,1... | collective-permute-start | bytes 589832 | tf_op jit(solution)/shard_map/ppermute | solution.py:16
  42.9 11.4 %collective-permute-start.7 = (bf16[768,128]{1,0:T(8,128)(2,1)S(1)}, bf16[768,128]{1,0:T(8,128)(2,1)S(1)}, u32[]{:S(2)}, u32[]{:S(2)}) collective-permute-start(bf16[768,128]{1,0:T(8,128)(2,1)S(1)} %all_gather.22), channel_id=1, source_target_pairs={{1,0},{2,1},{3,2},{4,3},{5,4},{6,5},{7,6},{0,7},{9,8},{10,9},{11,1... | collective-permute-start | bytes 589832 | tf_op jit(solution)/shard_map/ppermute | solution.py:18
  53.4 1.9 %copy-start.1 = (bf16[1,256,1024]{2,1,0:T(8,128)(2,1)S(1)}, bf16[1,256,1024]{2,1,0:T(8,128)(2,1)}, u32[]{:S(2)}) copy-start(bf16[1,256,1024]{2,1,0:T(8,128)(2,1)} %param.12) | copy-start | bytes 1572868
  55.6 7.8 %collective-permute-start.8 = (f32[1,256,128]{1,2,0:T(8,128)S(1)}, f32[1,256,128]{1,2,0:T(8,128)S(1)}, u32[]{:S(2)}, u32[]{:S(2)}) collective-permute-start(f32[1,256,128]{1,2,0:T(8,128)S(1)} %bitcast.115), channel_id=1, source_target_pairs={{0,1},{1,2},{2,3},{3,4},{4,5},{5,6},{6,7},{7,0},{8,9},{9,10},{10,1... | collective-permute-start | bytes 393224 | tf_op jit(solution)/shard_map/ppermute | solution.py:16
  56.0 7.8 %collective-permute-start.9 = (f32[1,256,128]{1,2,0:T(8,128)S(1)}, f32[1,256,128]{1,2,0:T(8,128)S(1)}, u32[]{:S(2)}, u32[]{:S(2)}) collective-permute-start(f32[1,256,128]{1,2,0:T(8,128)S(1)} %bitcast.116), channel_id=1, source_target_pairs={{1,0},{2,1},{3,2},{4,3},{5,4},{6,5},{7,6},{0,7},{9,8},{10,9},{11,1... | collective-permute-start | bytes 393224 | tf_op jit(solution)/shard_map/ppermute | solution.py:18
